TPU v7x, 256 devices: a whole 4x4x8 slice. The times are simulated.
256 devices in a mesh: row: 32 (over z, y), col: 8 (over x, core).
Axes of the slice: x: 4, y: 4, z: 8, core: 2. Of those that a mesh axis runs over, the one named last changes fastest.
Arguments:
- feats: bfloat16 [131072, 256], P(('row', 'col')), may hold values from -6 to 6
- w_msg: bfloat16 [256, 256], replicated, may hold values from -0.375 to 0.375
- w_self: bfloat16 [256, 256], replicated, may hold values from -0.375 to 0.375
- bias: float32 [256], replicated, may hold values from -3 to 3
- hit_mask: int32 [131072], P(('row', 'col')), may hold values 0 or 1
- block_cols: int32 [32, 8, 96], P('row', 'col'), may hold values from 0 to 127, as said below
- block_count: int32 [32, 8], P('row', 'col'), may hold values from 32 to 96, as said below
- edge_vals: bfloat16 [32, 8, 96, 128, 128], P('row', 'col'), may hold values from -0.125 to 0.125
- grad_out: bfloat16 [131072, 256], P(('row', 'col')), may hold values from -3 to 3
Outputs:
- hidden: bfloat16 [131072, 256], P(('row', 'col'))
- grad_feats: bfloat16 [131072, 256], P(('row', 'col'))
- edge_grad: bfloat16 [32, 8, 96, 128, 128], P('row', 'col')
- w_msg_grad: float32 [256, 256], replicated
- w_self_grad: float32 [256, 256], replicated
- bias_grad: float32 [256], replicated
Inputs may be any that keep to these rules, and one draw needn't show every extreme that they name: `block_cols`: slot s of a tile serves the tile's local block row s % 32; the block columns of the slots that serve one block row of one tile are different. Slots from block_count on are unused.
All inputs are finite; a program needn't handle non-finite values. No bound on the sum of `hit_mask` on one device may be relied on, other than what follows from the above.
Results may differ from a plain program's by a relative error of at most 0.015.
Values may be sent and summed in bfloat16 or wider, within the bound.
A program may use at most 128 MiB of HBM per device.

v0:
```python
import math
import jax
import jax.numpy as jnp
from jax import lax
from jax.sharding import PartitionSpec as P


def activate(pre, row_mask, grad_in):
    sig = jax.nn.sigmoid(pre)
    hidden = (pre * sig * row_mask).astype(jnp.bfloat16)
    deriv = sig * (1.0 + pre * (1.0 - sig))
    grad_pre = (grad_in.astype(jnp.float32) * row_mask * deriv).astype(jnp.bfloat16)
    return (hidden, grad_pre)


def per_device(feats, w_msg, w_self, bias, hit_mask, block_cols, block_count, edge_vals, grad_out):
    row_count = lax.axis_size("row")
    col_count = lax.axis_size("col")
    own_rows = feats.shape[0]
    width = feats.shape[1]
    row_mask = hit_mask.astype(jnp.float32)[:, None]
    messages = (jnp.dot(feats, w_msg, preferred_element_type=jnp.float32) * row_mask).astype(
        jnp.bfloat16
    )
    column_msgs = lax.all_gather(messages, "row", axis=0, tiled=True)
    slot_cols = block_cols[0, 0]
    edge_block = edge_vals[0, 0]
    slot_total = edge_block.shape[0]
    edge_size = edge_block.shape[1]
    tile_rows = col_count * own_rows // edge_size
    tile_cols = row_count * own_rows // edge_size
    slot_depth = slot_total // tile_rows
    slot_flags = jnp.arange(slot_total, dtype=jnp.int32) < block_count[0, 0]
    edge_live = (edge_block * slot_flags.astype(jnp.bfloat16)[:, None, None]).reshape(
        slot_depth, tile_rows, edge_size, edge_size
    )
    col_blocks = column_msgs.reshape(tile_cols, edge_size, width)[slot_cols].reshape(
        slot_depth, tile_rows, edge_size, width
    )
    partial_value = jnp.einsum(
        "krij,krjf->rif", edge_live, col_blocks, preferred_element_type=jnp.float32
    ).reshape(tile_rows * edge_size, width)
    summed = lax.psum_scatter(
        partial_value.astype(jnp.bfloat16), "col", scatter_dimension=0, tiled=True
    ).astype(jnp.float32)
    pre = summed + jnp.dot(feats, w_self, preferred_element_type=jnp.float32) + bias
    hidden, grad_pre = activate(pre, row_mask, grad_out)
    grad_rows_all = lax.all_gather(grad_pre, "col", axis=0, tiled=True)
    grad_tile = grad_rows_all.reshape(tile_rows, edge_size, width)
    backward = jnp.einsum(
        "krij,rif->krjf", edge_live, grad_tile, preferred_element_type=jnp.float32
    ).reshape(slot_total, edge_size, width)
    back_part = jax.ops.segment_sum(backward, slot_cols, num_segments=tile_cols).reshape(
        tile_cols * edge_size, width
    )
    edge_grad = (
        jnp.einsum(
            "rif,krjf->krij", grad_tile, col_blocks, preferred_element_type=jnp.float32
        ).reshape(slot_total, edge_size, edge_size)
        * slot_flags.astype(jnp.float32)[:, None, None]
    ).astype(jnp.bfloat16)
    grad_sum = lax.psum_scatter(
        back_part.astype(jnp.bfloat16), "row", scatter_dimension=0, tiled=True
    ).astype(jnp.float32)
    grad_msg = (grad_sum * row_mask).astype(jnp.bfloat16)
    grad_feats = (
        jnp.einsum("hg,fg->hf", grad_msg, w_msg, preferred_element_type=jnp.float32)
        + jnp.einsum("hg,fg->hf", grad_pre, w_self, preferred_element_type=jnp.float32)
    ).astype(jnp.bfloat16)
    local_msg = jnp.einsum("hf,hg->fg", feats, grad_msg, preferred_element_type=jnp.float32)
    local_self = jnp.einsum("hf,hg->fg", feats, grad_pre, preferred_element_type=jnp.float32)
    local_bias = jnp.sum(grad_pre.astype(jnp.float32), axis=0)
    total_msg, total_self, total_bias = lax.psum(
        (local_msg, local_self, local_bias), ("row", "col")
    )
    factor = 1.0 / math.sqrt(own_rows * row_count * col_count)
    return (
        hidden,
        grad_feats,
        edge_grad[None, None],
        total_msg * factor,
        total_self * factor,
        total_bias * factor,
    )


def solution(mesh):
    placed = (
        P(("row", "col"), None),
        P(),
        P(),
        P(),
        P(("row", "col")),
        P("row", "col", None),
        P("row", "col"),
        P("row", "col", None, None, None),
        P(("row", "col"), None),
    )
    return jax.shard_map(
        per_device,
        mesh=mesh,
        in_specs=placed,
        out_specs=(
            P(("row", "col"), None),
            P(("row", "col"), None),
            P("row", "col", None, None, None),
            P(),
            P(),
            P(),
        ),
        check_vma=False,
    )
```

profile of v0, /device:TPU:2, one launch (start us, length us, event | category | flops | bytes accessed | tf_op | source)
XLA Modules:
  0.0 757.9 jit_solution(17679265204071514697)
XLA Ops:
  7.2 0.7 convert_element_type.67
  7.9 0.2 copy-done
  8.1 1.8 fusion.12
  10.0 0.0 reduce-scatter.3.cloned.1.call-start
  10.7 0.7 fusion.16
  11.4 100.7 %all-gather.3.cloned.1.call-done = bf16[16384,256]{1,0:T(8,128)(2,1)} async-done(((bf16[512,256]{1,0:T(8,128)(2,1)}), bf16[16384,256]{1,0:T(8,128)(2,1)}) %all-gather.3.cloned.1.call-update) | async-done | bytes 8388624 | tf_op jit(solution)/shard_map/all_gather | solution.py:25
  112.0 9.5 %gather_fusion = bf16[96,128,256]{2,1,0:T(8,128)(2,1)} fusion(bf16[128,128,256]{2,1,0:T(8,128)(2,1)} %bitcast.53, s32[1024]{0:T(1024)S(1)} %pad_clamp_fusion), kind=kCustom, calls=%fused_computation | custom fusion | bytes 12583296 | tf_op jit(solution)/shard_map/gather | solution.py:37
  121.5 5.5 bitcast_convert_fusion
  127.0 0.0 all-gather.5.cloned.1.call-start
  127.1 30.4 %reduce-scatter.3.cloned.1.call-done = bf16[512,256]{1,0:T(8,128)(2,1)} async-done(((bf16[4096,256]{1,0:T(8,128)(2,1)}), bf16[512,256]{1,0:T(8,128)(2,1)}) %reduce-scatter.3.cloned.1.call-update) | async-done | bytes 262160 | tf_op jit(solution)/shard_map/reduce_scatter | solution.py:43
  157.5 2.3 convert_reduce_fusion
  159.8 0.0 reduce-scatter.5.cloned.1.call-start
  159.9 28.7 %all-gather.5.cloned.1.call-done = bf16[4096,256]{1,0:T(8,128)(2,1)} async-done(((bf16[512,256]{1,0:T(8,128)(2,1)}), bf16[4096,256]{1,0:T(8,128)(2,1)}) %all-gather.5.cloned.1.call-update) | async-done | bytes 2097168 | tf_op jit(solution)/shard_map/all_gather | solution.py:48
  188.6 8.0 %convolution_bitcast_fusion = f32[3,32,128,256]{2,3,0,1:T(8,128)} fusion(bf16[32,128,256,1]{2,1,3,0:T(8,128)(2,1)} %bitcast.51, bf16[3,32,128,128]{3,2,1,0:T(8,128)(2,1)S(1)} %bitcast.55, bf16[3,32]{0,1:T(8,128)(2,1)S(1)} %fusion.15), kind=kOutput, calls=%fused_computation.7 | convolution fusion | flops 811597824 | bytes 17825984 | tf_op jit(solution)/shard_map/krij,rif->krjf/dot_general | solution.py:50
  196.6 12.6 %copy.22 = f32[3,32,128,256]{3,2,1,0:T(8,128)} copy(f32[3,32,128,256]{2,3,0,1:T(8,128)} %convolution_bitcast_fusion) | data formatting | bytes 25165824 | tf_op jit(solution)/shard_map/krij,rif->krjf/transpose | solution.py:50
  209.2 7.8 %broadcast_in_dim.2 = f32[128,128,256]{2,1,0:T(8,128)} broadcast(f32[]{:T(128)} %constant.4.clone.1), dimensions={} | broadcast | bytes 16777220 | tf_op jit(solution)/shard_map/broadcast_in_dim | solution.py:53
  217.0 29.1 %scatter_fusion = f32[128,128,256]{2,1,0:T(8,128)} fusion(f32[128,128,256]{2,1,0:T(8,128)} %broadcast_in_dim.2, s32[96]{0:T(128)S(1)} %bitcast.57, f32[96,128,256]{2,1,0:T(8,128)} %bitcast.46), kind=kCustom, calls=%fused_computation.1 | custom fusion | flops 3145728 | bytes 37749120 | tf_op jit(solution)/shard_map/scatter-add | solution.py:53
  246.1 9.0 %convert_element_type.75 = bf16[128,128,256]{2,1,0:T(8,128)(2,1)} convert(f32[128,128,256]{2,1,0:T(8,128)} %scatter_fusion) | non-fusion elementwise | flops 4194304 | bytes 25165824 | tf_op jit(solution)/shard_map/convert_element_type | solution.py:63
  255.2 78.1 %psum.23 = f32[256]{0:T(256)S(1)} all-reduce(f32[256]{0:T(256)S(1)} %get-tuple-element.20), channel_id=1, replica_groups=mesh['row'=32,'col'=8] {'row','col'}, use_global_device_ids=true, to_apply=%region_6.0 | all-reduce | flops 256 | bytes 2048 | tf_op jit(solution)/shard_map/psum | solution.py:73
  333.3 0.6 broadcast_multiply_fusion.2
  333.9 1.0 convolution_bitcast_fusion.1
  334.9 7.3 fusion.4
  342.1 6.6 copy.24
  348.7 5.1 multiply_convert_fusion
  353.8 134.4 %reduce-scatter.5.cloned.1.call-done = bf16[512,256]{1,0:T(8,128)(2,1)} async-done(((bf16[16384,256]{1,0:T(8,128)(2,1)}), bf16[512,256]{1,0:T(8,128)(2,1)}) %reduce-scatter.5.cloned.1.call-update) | async-done | bytes 262160 | tf_op jit(solution)/shard_map/reduce_scatter | solution.py:62
  488.2 2.0 convolution_bitcast_fusion.2
  490.2 1.2 fusion.14
  491.4 1.0 fusion.13
  492.4 256.2 %all-reduce.3.cloned.1.call-done = (f32[256,256]{0,1:T(8,128)}, f32[256,256]{0,1:T(8,128)}) async-done(((f32[256,256]{0,1:T(8,128)}, f32[256,256]{0,1:T(8,128)}), (f32[256,256]{0,1:T(8,128)}, f32[256,256]{0,1:T(8,128)})) %all-reduce.3.cloned.1.call-update) | async-done | bytes 524304 | tf_op jit(solution)/shard_map/psum | solution.py:73
  748.6 1.1 broadcast_multiply_fusion
  749.7 0.8 copy.26
  750.5 0.8 copy.25
  (23 shorter events, 0.2 us)
Async XLA Ops:
  7.2 1.0 copy-start
  7.2 104.8 %all-gather.3.cloned.1.call-start = ((), (), s32[]{:S(2)}) async-start(), calls=%async_computation.2 | async-start | bytes 8650752 | tf_op jit(solution)/shard_map/all_gather | solution.py:25
  10.0 147.5 %reduce-scatter.3.cloned.1.call-start = ((), (), s32[]{:S(2)}) async-start(), calls=%async_computation.3 | async-start | bytes 2359296 | tf_op jit(solution)/shard_map/reduce_scatter | solution.py:43
  112.0 9.5 %copy-start.2 = (bf16[1,1,96,128,128]{4,3,2,1,0:T(8,128)(2,1)S(1)}, bf16[1,1,96,128,128]{4,3,2,1,0:T(8,128)(2,1)}, u32[]{:S(2)}) copy-start(bf16[1,1,96,128,128]{4,3,2,1,0:T(8,128)(2,1)} %param.16) | copy-start | bytes 9437188
  121.5 36.0 %copy-start.5 = (bf16[256,256]{1,0:T(8,128)(2,1)S(1)}, bf16[256,256]{1,0:T(8,128)(2,1)}, u32[]{:S(2)}) copy-start(bf16[256,256]{1,0:T(8,128)(2,1)} %param.11) | copy-start | bytes 393220
  127.0 61.6 %all-gather.5.cloned.1.call-start = ((), (), s32[]{:S(2)}) async-start(), calls=%async_computation.4 | async-start | bytes 2359296 | tf_op jit(solution)/shard_map/all_gather | solution.py:48
  159.8 328.4 %reduce-scatter.5.cloned.1.call-start = ((), (), s32[]{:S(2)}) async-start(), calls=%async_computation.5 | async-start | bytes 8650752 | tf_op jit(solution)/shard_map/reduce_scatter | solution.py:62
  209.2 7.9 %copy-start.6 = (s32[1,1,96]{2,1,0:T(1,128)S(1)}, s32[1,1,96]{2,1,0:T(1,128)}, u32[]{:S(2)}) copy-start(s32[1,1,96]{2,1,0:T(1,128)} %param.14) | copy-start | bytes 1156
  255.1 78.7 %copy-start.3 = (bf16[512,256]{1,0:T(8,128)(2,1)S(1)}, bf16[512,256]{1,0:T(8,128)(2,1)}, u32[]{:S(2)}) copy-start(bf16[512,256]{1,0:T(8,128)(2,1)} %get-tuple-element.21) | copy-start | bytes 786436
  255.1 79.7 %copy-start.1 = (bf16[4096,256]{1,0:T(8,128)(2,1)S(1)}, bf16[4096,256]{1,0:T(8,128)(2,1)}, u32[]{:S(2)}) copy-start(bf16[4096,256]{1,0:T(8,128)(2,1)} %all-gather.5.cloned.1.call-done) | copy-start | bytes 6291460
  255.2 493.4 %all-reduce.3.cloned.1.call-start = ((), (), s32[]{:S(2)}) async-start(), calls=%async_computation.6 | async-start | bytes 1048576 | tf_op jit(solution)/shard_map/psum | solution.py:73
  348.7 141.5 %copy-start.4 = (bf16[256,256]{1,0:T(8,128)(2,1)S(1)}, bf16[256,256]{1,0:T(8,128)(2,1)}, u32[]{:S(2)}) copy-start(bf16[256,256]{1,0:T(8,128)(2,1)} %param.10) | copy-start | bytes 393220
Sparse Core Ops, SparseCore 0:
  11.1 100.8 all-gather.2
  127.1 30.3 reduce-scatter.2
  159.9 28.6 all-gather.4
  255.3 232.8 reduce-scatter.4
  494.2 254.3 all-reduce.2
where the time goes:
time: 758 us
  waiting for transfers between devices  550 us (73%)
  blocking collectives  78.1 us (10%)
  other arithmetic  46.2 us (6%)
  local copies, waits for them, and re-layouts  38.4 us (5%)
  matrix products  30 us (4%)
  between operations  14.5 us (2%)
    psum x1, waiting for transfers between devices, per_device(): lax.psum((local_msg, local_self, local_bias), ('row', 'col'))  256 us
    reduce_scatter x1, waiting for transfers between devices, per_device(): lax.psum_scatter(back_part.astype(jnp.bfloat16), 'row', scatter_dimension...  134 us
    all_gather x1, waiting for transfers between devices, per_device(): column_msgs = lax.all_gather(messages, 'row', axis=0, tiled=True)  101 us
    psum x1, blocking collectives, per_device(): lax.psum((local_msg, local_self, local_bias), ('row', 'col'))  78.1 us
    reduce_scatter x1, waiting for transfers between devices, per_device(): lax.psum_scatter(partial_value.astype(jnp.bfloat16), 'col', scatter_dimen...  30.4 us
    scatter-add x1, other arithmetic, per_device(): jax.ops.segment_sum(backward, slot_cols, num_segments=tile_cols)  29.1 us
    all_gather x1, waiting for transfers between devices, per_device(): grad_rows_all = lax.all_gather(grad_pre, 'col', axis=0, tiled=True)  28.7 us
  transfers between devices with their start and end apart: 5, of which 5 were waited for; matrix products, arithmetic and copies ran while one was open for 3% of the time, Pallas kernels for 0%

commit v1 on v0

--- a/solution.py
+++ b/solution.py
@@ -71,7 +71,7 @@
     local_self = jnp.einsum("hf,hg->fg", feats, grad_pre, preferred_element_type=jnp.float32)
     local_bias = jnp.sum(grad_pre.astype(jnp.float32), axis=0)
     total_msg, total_self, total_bias = lax.psum(
-        (local_msg, local_self, local_bias), ("row", "col")
+        lax.psum((local_msg, local_self, local_bias), "col"), "row"
     )
     factor = 1.0 / math.sqrt(own_rows * row_count * col_count)
     return (

time: 758 us -> 717 us (0.946)
  waiting for transfers between devices: 550 us -> 501 us
  blocking collectives: 78.1 us -> 87 us
    psum x1 -> x2, waiting for transfers between devices: 256 us -> 197 us  [the longest x1 147 us: per_device(): lax.psum(lax.psum((local_msg, local_self, local_bias), 'col'), 'row')]
    reduce_scatter x1, waiting for transfers between devices: 134 us -> 144 us  [per_device(): lax.psum_scatter(back_part.astype(jnp.bfloat16), 'row', scatter_dimension...]
    psum x1 -> x2, blocking collectives: 78.1 us -> 87 us  [the longest x1 75 us: per_device(): lax.psum(lax.psum((local_msg, local_self, local_bias), 'col'), 'row')]
  transfers between devices with their start and end apart: 5 -> 6, of which waited for: 5 -> 6; matrix products, arithmetic and copies ran while one was open for 3% -> 3% of each run, Pallas kernels for 0% -> 0%
where the time goes in v1:
time: 717 us; the launch traced here: 716 us
  waiting for transfers between devices  501 us (70%)
  blocking collectives  87 us (12%)
  other arithmetic  46.2 us (6%)
  local copies, waits for them, and re-layouts  38.4 us (5%)
  matrix products  29 us (4%)
  between operations  14.8 us (2%)
    psum x1, waiting for transfers between devices, per_device(): lax.psum(lax.psum((local_msg, local_self, local_bias), 'col'), 'row')  147 us
    reduce_scatter x1, waiting for transfers between devices, per_device(): lax.psum_scatter(back_part.astype(jnp.bfloat16), 'row', scatter_dimension...  144 us
    all_gather x1, waiting for transfers between devices, per_device(): column_msgs = lax.all_gather(messages, 'row', axis=0, tiled=True)  101 us
    psum x1, blocking collectives, per_device(): lax.psum(lax.psum((local_msg, local_self, local_bias), 'col'), 'row')  75 us
    psum x1, waiting for transfers between devices, per_device(): lax.psum((local_msg, local_self, local_bias), 'col')  49.3 us
    reduce_scatter x1, waiting for transfers between devices, per_device(): lax.psum_scatter(partial_value.astype(jnp.bfloat16), 'col', scatter_dimen...  30.4 us
    scatter-add x1, other arithmetic, per_device(): jax.ops.segment_sum(backward, slot_cols, num_segments=tile_cols)  29.1 us
    all_gather x1, waiting for transfers between devices, per_device(): grad_rows_all = lax.all_gather(grad_pre, 'col', axis=0, tiled=True)  28.7 us
  transfers between devices with their start and end apart: 6, of which 6 were waited for; matrix products, arithmetic and copies ran while one was open for 3% of the time, Pallas kernels for 0%

profile of v1, /device:TPU:2, one launch (start us, length us, event | category | flops | bytes accessed | tf_op | source)
XLA Modules:
  0.0 716.3 jit_solution(9305779169490277103)
XLA Ops:
  7.2 0.7 convert_element_type.67
  7.9 0.2 copy-done
  8.1 1.8 fusion.12
  10.7 0.7 fusion.16
  11.4 100.7 %all-gather.3.cloned.1.call-done = bf16[16384,256]{1,0:T(8,128)(2,1)} async-done(((bf16[512,256]{1,0:T(8,128)(2,1)}), bf16[16384,256]{1,0:T(8,128)(2,1)}) %all-gather.3.cloned.1.call-update) | async-done | bytes 8388624 | tf_op jit(solution)/shard_map/all_gather | solution.py:25
  112.0 9.5 %gather_fusion = bf16[96,128,256]{2,1,0:T(8,128)(2,1)} fusion(bf16[128,128,256]{2,1,0:T(8,128)(2,1)} %bitcast.53, s32[1024]{0:T(1024)S(1)} %pad_clamp_fusion), kind=kCustom, calls=%fused_computation | custom fusion | bytes 12583296 | tf_op jit(solution)/shard_map/gather | solution.py:37
  121.5 5.5 bitcast_convert_fusion
  127.1 30.4 %reduce-scatter.3.cloned.1.call-done = bf16[512,256]{1,0:T(8,128)(2,1)} async-done(((bf16[4096,256]{1,0:T(8,128)(2,1)}), bf16[512,256]{1,0:T(8,128)(2,1)}) %reduce-scatter.3.cloned.1.call-update) | async-done | bytes 262160 | tf_op jit(solution)/shard_map/reduce_scatter | solution.py:43
  157.5 2.3 convert_reduce_fusion
  159.9 28.7 %all-gather.5.cloned.1.call-done = bf16[4096,256]{1,0:T(8,128)(2,1)} async-done(((bf16[512,256]{1,0:T(8,128)(2,1)}), bf16[4096,256]{1,0:T(8,128)(2,1)}) %all-gather.5.cloned.1.call-update) | async-done | bytes 2097168 | tf_op jit(solution)/shard_map/all_gather | solution.py:48
  188.6 8.0 %convolution_bitcast_fusion = f32[3,32,128,256]{2,3,0,1:T(8,128)} fusion(bf16[32,128,256,1]{2,1,3,0:T(8,128)(2,1)} %bitcast.51, bf16[3,32,128,128]{3,2,1,0:T(8,128)(2,1)S(1)} %bitcast.55, bf16[3,32]{0,1:T(8,128)(2,1)S(1)} %fusion.15), kind=kOutput, calls=%fused_computation.7 | convolution fusion | flops 811597824 | bytes 17825984 | tf_op jit(solution)/shard_map/krij,rif->krjf/dot_general | solution.py:50
  196.6 12.6 %copy.22 = f32[3,32,128,256]{3,2,1,0:T(8,128)} copy(f32[3,32,128,256]{2,3,0,1:T(8,128)} %convolution_bitcast_fusion) | data formatting | bytes 25165824 | tf_op jit(solution)/shard_map/krij,rif->krjf/transpose | solution.py:50
  209.2 7.8 %broadcast_in_dim.2 = f32[128,128,256]{2,1,0:T(8,128)} broadcast(f32[]{:T(128)} %constant.4.clone.1), dimensions={} | broadcast | bytes 16777220 | tf_op jit(solution)/shard_map/broadcast_in_dim | solution.py:53
  217.0 29.1 %scatter_fusion = f32[128,128,256]{2,1,0:T(8,128)} fusion(f32[128,128,256]{2,1,0:T(8,128)} %broadcast_in_dim.2, s32[96]{0:T(128)S(1)} %bitcast.57, f32[96,128,256]{2,1,0:T(8,128)} %bitcast.46), kind=kCustom, calls=%fused_computation.1 | custom fusion | flops 3145728 | bytes 37749120 | tf_op jit(solution)/shard_map/scatter-add | solution.py:53
  246.1 9.0 %convert_element_type.75 = bf16[128,128,256]{2,1,0:T(8,128)(2,1)} convert(f32[128,128,256]{2,1,0:T(8,128)} %scatter_fusion) | non-fusion elementwise | flops 4194304 | bytes 25165824 | tf_op jit(solution)/shard_map/convert_element_type | solution.py:63
  255.2 12.0 %psum.46 = f32[256]{0:T(256)S(1)} all-reduce(f32[256]{0:T(256)S(1)} %get-tuple-element.22), channel_id=1, replica_groups=mesh['row'=32,'col'=8] {'col'}, use_global_device_ids=true, to_apply=%region_8.0 | all-reduce | flops 256 | bytes 2048 | tf_op jit(solution)/shard_map/psum | solution.py:74
  267.2 75.0 %psum.47 = f32[256]{0:T(256)S(1)} all-reduce(f32[256]{0:T(256)S(1)} %psum.46), channel_id=1, replica_groups=mesh['row'=32,'col'=8] {'row'}, use_global_device_ids=true, to_apply=%region_9.0 | all-reduce | flops 256 | bytes 2048 | tf_op jit(solution)/shard_map/psum | solution.py:73
  342.2 0.6 broadcast_multiply_fusion.2
  342.8 1.0 convolution_bitcast_fusion.1
  343.8 144.1 %reduce-scatter.5.cloned.1.call-done = bf16[512,256]{1,0:T(8,128)(2,1)} async-done(((bf16[16384,256]{1,0:T(8,128)(2,1)}), bf16[512,256]{1,0:T(8,128)(2,1)}) %reduce-scatter.5.cloned.1.call-update) | async-done | bytes 262160 | tf_op jit(solution)/shard_map/reduce_scatter | solution.py:62
  487.8 2.0 convolution_bitcast_fusion.2
  489.9 0.2 all-reduce.5.cloned.1.call-start
  490.1 7.2 %fusion.4 = f32[3,32,128,128]{2,3,0,1:T(8,128)} fusion(bf16[32,128,256,1]{2,1,3,0:T(8,128)(2,1)S(1)} %bitcast.52, bf16[3,32,128,256]{3,2,1,0:T(8,128)(2,1)} %bitcast.49), kind=kOutput, calls=%fused_computation.10 | convolution fusion | flops 805306368 | bytes 14680064 | tf_op jit(solution)/shard_map/rif,krjf->krij/dot_general | solution.py:57
  497.3 6.5 copy.24
  503.9 49.3 %all-reduce.7.cloned.1.call-done = (f32[256,256]{0,1:T(8,128)}, f32[256,256]{0,1:T(8,128)}) async-done(((f32[256,256]{0,1:T(8,128)}, f32[256,256]{0,1:T(8,128)}), (f32[256,256]{0,1:T(8,128)}, f32[256,256]{0,1:T(8,128)})) %all-reduce.7.cloned.1.call-update) | async-done | bytes 524304 | tf_op jit(solution)/shard_map/psum | solution.py:74
  553.1 5.0 multiply_convert_fusion
  558.2 0.3 fusion.14
  558.4 1.0 fusion.13
  559.4 147.3 %all-reduce.5.cloned.1.call-done = (f32[256,256]{0,1:T(8,128)}, f32[256,256]{0,1:T(8,128)}) async-done(((f32[256,256]{0,1:T(8,128)}, f32[256,256]{0,1:T(8,128)}), (f32[256,256]{0,1:T(8,128)}, f32[256,256]{0,1:T(8,128)})) %all-reduce.5.cloned.1.call-update) | async-done | bytes 524304 | tf_op jit(solution)/shard_map/psum | solution.py:73
  706.7 1.1 broadcast_multiply_fusion
  707.8 0.8 copy.26
  708.6 0.8 copy.25
  (29 shorter events, 0.4 us)
Async XLA Ops:
  7.2 1.0 copy-start
  7.2 104.8 %all-gather.3.cloned.1.call-start = ((), (), s32[]{:S(2)}) async-start(), calls=%async_computation.2 | async-start | bytes 8650752 | tf_op jit(solution)/shard_map/all_gather | solution.py:25
  10.0 147.5 %reduce-scatter.3.cloned.1.call-start = ((), (), s32[]{:S(2)}) async-start(), calls=%async_computation.3 | async-start | bytes 2359296 | tf_op jit(solution)/shard_map/reduce_scatter | solution.py:43
  112.0 9.5 %copy-start.2 = (bf16[1,1,96,128,128]{4,3,2,1,0:T(8,128)(2,1)S(1)}, bf16[1,1,96,128,128]{4,3,2,1,0:T(8,128)(2,1)}, u32[]{:S(2)}) copy-start(bf16[1,1,96,128,128]{4,3,2,1,0:T(8,128)(2,1)} %param.16) | copy-start | bytes 9437188
  121.5 36.0 %copy-start.6 = (bf16[256,256]{1,0:T(8,128)(2,1)S(1)}, bf16[256,256]{1,0:T(8,128)(2,1)}, u32[]{:S(2)}) copy-start(bf16[256,256]{1,0:T(8,128)(2,1)} %param.11) | copy-start | bytes 393220
  127.0 61.6 %all-gather.5.cloned.1.call-start = ((), (), s32[]{:S(2)}) async-start(), calls=%async_computation.4 | async-start | bytes 2359296 | tf_op jit(solution)/shard_map/all_gather | solution.py:48
  159.8 328.0 %reduce-scatter.5.cloned.1.call-start = ((), (), s32[]{:S(2)}) async-start(), calls=%async_computation.5 | async-start | bytes 8650752 | tf_op jit(solution)/shard_map/reduce_scatter | solution.py:62
  209.2 7.9 %copy-start.7 = (s32[1,1,96]{2,1,0:T(1,128)S(1)}, s32[1,1,96]{2,1,0:T(1,128)}, u32[]{:S(2)}) copy-start(s32[1,1,96]{2,1,0:T(1,128)} %param.14) | copy-start | bytes 1156
  255.1 87.6 %copy-start.3 = (bf16[512,256]{1,0:T(8,128)(2,1)S(1)}, bf16[512,256]{1,0:T(8,128)(2,1)}, u32[]{:S(2)}) copy-start(bf16[512,256]{1,0:T(8,128)(2,1)} %get-tuple-element.23) | copy-start | bytes 786436
  255.1 235.0 %copy-start.1 = (bf16[4096,256]{1,0:T(8,128)(2,1)S(1)}, bf16[4096,256]{1,0:T(8,128)(2,1)}, u32[]{:S(2)}) copy-start(bf16[4096,256]{1,0:T(8,128)(2,1)} %all-gather.5.cloned.1.call-done) | copy-start | bytes 6291460
  255.2 297.9 %all-reduce.7.cloned.1.call-start = ((), (), s32[]{:S(2)}) async-start(), calls=%async_computation.7 | async-start | bytes 1048576 | tf_op jit(solution)/shard_map/psum | solution.py:74
  489.9 216.8 %all-reduce.5.cloned.1.call-start = ((), (), s32[]{:S(2)}) async-start(), calls=%async_computation.6 | async-start | bytes 1048576 | tf_op jit(solution)/shard_map/psum | solution.py:73
  503.8 54.3 %copy-start.4 = (bf16[512,256]{1,0:T(8,128)(2,1)S(1)}, bf16[512,256]{1,0:T(8,128)(2,1)}, u32[]{:S(2)}) copy-start(bf16[512,256]{1,0:T(8,128)(2,1)} %reduce-scatter.5.cloned.1.call-done) | copy-start | bytes 786436
  503.8 54.3 %copy-start.5 = (bf16[256,256]{1,0:T(8,128)(2,1)S(1)}, bf16[256,256]{1,0:T(8,128)(2,1)}, u32[]{:S(2)}) copy-start(bf16[256,256]{1,0:T(8,128)(2,1)} %param.10) | copy-start | bytes 393220
Sparse Core Ops, SparseCore 0:
  11.1 100.8 all-gather.2
  127.1 30.3 reduce-scatter.2
  159.9 28.6 all-gather.4
  255.3 232.4 reduce-scatter.4
  490.7 62.4 all-reduce.6
  556.4 150.2 all-reduce.4
